TPU v7x, 256 devices: a whole 4x4x8 slice. The times are simulated.
256 devices in a mesh: wide: 64 (over y, z, core), narrow: 4 (over x).
Axes of the slice: x: 4, y: 4, z: 8, core: 2. Of those that a mesh axis runs over, the one named last changes fastest.
Arguments:
- patches: bfloat16 [65536, 1280], P('wide', 'narrow'), may hold values from -6 to 6
- norm_gain: float32 [1280], replicated, may hold values from 0.1 to 1.9
- norm_bias: float32 [1280], replicated, may hold values from -3 to 3
- w_in: bfloat16 [1280, 5120], P('wide', 'narrow'), may hold values from -0.15625 to 0.15625
- b_in: float32 [5120], P('narrow'), may hold values from -3 to 3
- w_out: bfloat16 [5120, 1280], P('narrow', 'wide'), may hold values from -0.078125 to 0.078125
- b_out: float32 [1280], P('narrow'), may hold values from -3 to 3
- w_proj: bfloat16 [4, 1280, 1280], P(None, 'narrow', 'wide'), may hold values from -0.078125 to 0.078125
- b_proj: float32 [1280], P('narrow'), may hold values from -3 to 3
- text: bfloat16 [32768, 1280], P('wide', 'narrow'), may hold values from -6 to 6
- place: int32 [16384], replicated, may hold values from -1 to 32767, as said below
Outputs:
- prompt_embeds: bfloat16 [32768, 1280], P('wide', 'narrow')
Inputs may be any that keep to these rules, and one draw needn't show every extreme that they name: `place`: of the 256 entries of one wide index (entries i * 256 to (i + 1) * 256 - 1), the valid ones (>= 0) come first and -1 fills the rest; three quarters or more are valid, and all are valid for some wide index. Valid values are distinct. For one wide index, at most 8 valid entries v have the same v // 512, and every wide index reaches 8 for some value.
All inputs are finite; a program needn't handle non-finite values.
Results may differ from a plain program's by a relative error of at most 0.012.
Values may be sent and summed in bfloat16 or wider, within the bound.
A program may use at most 64 MiB of HBM per device.

v0:
```python
import jax
import jax.numpy as jnp
from jax import lax
from jax.sharding import PartitionSpec as P


def per_device(
    patches, norm_gain, norm_bias, w_in, b_in, w_out, b_out, w_proj, b_proj, text, place
):
    whole = lax.all_gather(patches, "narrow", axis=1, tiled=True)
    values = whole.astype(jnp.float32)
    center = jnp.mean(values, axis=-1, keepdims=True)
    spread = jnp.mean(jnp.square(values - center), axis=-1, keepdims=True)
    normed = ((values - center) * lax.rsqrt(spread + 1e-06) * norm_gain + norm_bias).astype(
        jnp.bfloat16
    )
    rows_in, cols_out, proj_cols = (
        lax.all_gather(w_in, "wide", axis=0, tiled=True),
        lax.all_gather(w_out, "wide", axis=1, tiled=True),
        lax.all_gather(w_proj, "wide", axis=2, tiled=True),
    )
    product = jnp.dot(normed, rows_in, preferred_element_type=jnp.float32)
    hidden = jax.nn.gelu(product + b_in, approximate=False).astype(jnp.bfloat16)
    partial_out = jnp.dot(hidden, cols_out, preferred_element_type=jnp.float32)
    mlp_out = lax.psum_scatter(
        partial_out.astype(jnp.bfloat16), "narrow", scatter_dimension=1, tiled=True
    ).astype(jnp.float32)
    stream = (patches.astype(jnp.float32) + (mlp_out + b_out)).astype(jnp.bfloat16)
    merge_count = stream.shape[0] // 4
    merged = stream.reshape(merge_count, 4 * stream.shape[1])
    groups = lax.axis_size("wide")
    own_index = lax.axis_index("wide")
    seq_rows = text.shape[0]
    bucket = seq_rows // groups
    place_table = place.reshape(groups, merge_count)
    owners = jnp.where(place_table >= 0, place_table // seq_rows, groups)
    own_owners = lax.dynamic_index_in_dim(owners, own_index, 0, keepdims=False)
    owner_hits = (own_owners[:, None] == jnp.arange(groups, dtype=jnp.int32)[None, :]).astype(
        jnp.int32
    )
    slot_out = jnp.sum(jnp.cumsum(owner_hits, axis=0) * owner_hits, axis=1) - 1
    slot_out = jnp.where(own_owners < groups, slot_out, bucket)
    arriving = owners == own_index
    slot_in = jnp.cumsum(arriving.astype(jnp.int32), axis=1) - 1
    slot_in = jnp.where(arriving, slot_in, bucket)
    local_row = jnp.where(arriving, place_table % seq_rows, seq_rows)
    source_ids = jnp.arange(groups, dtype=jnp.int32)[:, None]
    targets = (
        jnp.full((groups, bucket), seq_rows, jnp.int32)
        .at[source_ids, slot_in]
        .set(local_row, mode="drop")
    )
    partial_proj = jnp.dot(
        merged, proj_cols.reshape(-1, proj_cols.shape[2]), preferred_element_type=jnp.float32
    )
    vision = (
        lax.psum_scatter(
            partial_proj.astype(jnp.bfloat16), "narrow", scatter_dimension=1, tiled=True
        ).astype(jnp.float32)
        + b_proj
    ).astype(jnp.bfloat16)
    buffer = jnp.zeros((groups, bucket, vision.shape[1]), vision.dtype)
    received = lax.all_to_all(
        buffer.at[own_owners, slot_out].set(vision, mode="drop"),
        "wide",
        split_axis=0,
        concat_axis=0,
        tiled=True,
    )
    return text.at[targets.reshape(-1)].set(received.reshape(-1, received.shape[2]), mode="drop")


def solution(mesh):
    placed = (
        P("wide", "narrow"),
        P(),
        P(),
        P("wide", "narrow"),
        P("narrow"),
        P("narrow", "wide"),
        P("narrow"),
        P(None, "narrow", "wide"),
        P("narrow"),
        P("wide", "narrow"),
        P(),
    )
    return jax.shard_map(
        per_device, mesh=mesh, in_specs=placed, out_specs=P("wide", "narrow"), check_vma=False
    )
```

profile of v0, /device:TPU:1, one launch (start us, length us, event | category | flops | bytes accessed | tf_op | source)
XLA Modules:
  0.0 475.5 jit_solution(18074952579770676036)
XLA Ops:
  6.5 0.0 all-gather.7.cloned.1.call-start
  6.5 0.7 all-gather.7.cloned.1.call-update
  7.3 0.0 all-gather.13.cloned.1.call-start
  7.3 0.7 all-gather.13.cloned.1.call-update
  8.0 0.0 all-gather.11.cloned.1.call-start
  8.1 0.7 all-gather.11.cloned.1.call-update
  8.7 0.0 all-gather.9.cloned.1.call-start
  8.8 0.5 all-gather.9.cloned.1.call-update
  9.3 0.0 reduce-scatter.3.cloned.1.call-start
  9.4 41.4 %all-gather.7.cloned.1.call-done = bf16[1024,1280]{0,1:T(8,128)(2,1)} async-done(((bf16[1024,320]{0,1:T(8,128)(2,1)}), bf16[1024,1280]{0,1:T(8,128)(2,1)}) %all-gather.7.cloned.1.call-update) | async-done | bytes 2621456 | tf_op jit(solution)/shard_map/all_gather | solution.py:10
  50.7 2.3 convert_reduce_fusion
  53.1 0.2 copy-done
  53.2 0.7 fusion.2
  54.0 78.9 %all-gather.13.cloned.1.call-done = bf16[64,20,1280]{2,1,0:T(8,128)(2,1)} async-done(((bf16[1,20,1280]{2,1,0:T(8,128)(2,1)}), bf16[64,20,1280]{2,1,0:T(8,128)(2,1)}) %all-gather.13.cloned.1.call-update) | async-done | bytes 3276816 | tf_op jit(solution)/shard_map/all_gather | solution.py:19
  132.9 6.1 %reshape.317 = bf16[1280,1280]{1,0:T(8,128)(2,1)} reshape(bf16[64,20,1280]{2,1,0:T(8,128)(2,1)} %all-gather.13.cloned.1.call-done) | data formatting | bytes 6553600
  139.1 72.6 %all-gather.11.cloned.1.call-done = bf16[64,20,1280]{2,1,0:T(8,128)(2,1)} async-done(((bf16[1,20,1280]{2,1,0:T(8,128)(2,1)}), bf16[64,20,1280]{2,1,0:T(8,128)(2,1)}) %all-gather.11.cloned.1.call-update) | async-done | bytes 3276816 | tf_op jit(solution)/shard_map/all_gather | solution.py:18
  211.7 6.1 %reshape.315 = bf16[1280,1280]{1,0:T(8,128)(2,1)} reshape(bf16[64,20,1280]{2,1,0:T(8,128)(2,1)} %all-gather.11.cloned.1.call-done) | data formatting | bytes 6553600
  217.8 0.0 copy-done.6
  217.8 0.0 copy-done.7
  217.8 0.0 copy-done.8
  217.8 0.0 copy-start.1
  217.8 21.4 %convolution_convert_fusion = bf16[1024,1280]{0,1:T(8,128)(2,1)} fusion(bf16[1280,1280]{1,0:T(8,128)(2,1)} %reshape.317, bf16[1280,1280]{1,0:T(8,128)(2,1)} %reshape.315, bf16[1024,1280]{0,1:T(8,128)(2,1)S(1)} %copy-done, f32[1280]{0:T(1024)S(1)} %copy-done.6, f32[1280]{0:T(1024)S(1)} %copy-done.7, f32[1280]{0:T(1024)S(1)} %copy-done.8, ...), kind=kOutput, calls=%fused_computation.30 | convolution fusion | flops 6806568960 | bytes 11820032 | tf_op jit(solution)/shard_map/dot_general | solution.py:24
  239.2 0.0 reduce-scatter.3.cloned.1.call-update
  239.2 0.0 copy-start.2
  239.3 0.0 reduce-scatter.5.cloned.1.call-start
  239.3 0.0 copy-done.1
  239.4 0.1 fusion.40
  239.4 0.6 reduce-window.14
  240.0 0.2 slice_reduce_fusion.1
  240.3 0.1 add_add_fusion
  240.4 49.9 %all-gather.9.cloned.1.call-done = bf16[4,320,1280]{1,0,2:T(4,128)(2,1)} async-done(((bf16[4,320,20]{1,0,2:T(4,128)(2,1)}), bf16[4,320,1280]{1,0,2:T(4,128)(2,1)}) %all-gather.9.cloned.1.call-update) | async-done | bytes 3276816 | tf_op jit(solution)/shard_map/all_gather | solution.py:20
  290.3 7.3 %copy.46 = bf16[4,320,1280]{2,1,0:T(8,128)(2,1)S(1)} copy(bf16[4,320,1280]{1,0,2:T(4,128)(2,1)} %all-gather.9.cloned.1.call-done) | data formatting | bytes 6553600 | tf_op jit(solution)/shard_map/all_gather | solution.py:20
  297.6 28.3 %reduce-scatter.3.cloned.1.call-done = bf16[1024,320]{0,1:T(8,128)(2,1)} async-done(((bf16[1024,1280]{0,1:T(8,128)(2,1)}), bf16[1024,320]{0,1:T(8,128)(2,1)}) %reduce-scatter.3.cloned.1.call-update) | async-done | bytes 655376 | tf_op jit(solution)/shard_map/reduce_scatter | solution.py:25
  326.0 0.0 copy-done.2
  326.0 2.4 add_convert_fusion
  328.4 2.2 copy.45
  330.6 2.5 reshape.287
  333.1 3.3 convolution_convert_fusion.1
  336.4 0.0 reduce-scatter.5.cloned.1.call-update
  336.4 0.1 fusion.31
  336.5 1.2 copy.48
  337.7 0.1 copy.42
  337.8 0.1 sub.37
  337.9 0.6 reduce-window.16
  338.5 0.2 slice_reduce_fusion
  338.7 0.1 fusion.35
  338.9 0.1 compare_select_fusion
  338.9 20.6 %reduce-scatter.5.cloned.1.call-done = bf16[256,320]{0,1:T(8,128)(2,1)} async-done(((bf16[256,1280]{0,1:T(8,128)(2,1)}), bf16[256,320]{0,1:T(8,128)(2,1)}) %reduce-scatter.5.cloned.1.call-update) | async-done | bytes 163856 | tf_op jit(solution)/shard_map/reduce_scatter | solution.py:57
  359.5 0.0 copy-done.3
  359.5 1.0 add_convert_fusion.1
  360.5 0.2 copy.47
  360.7 0.8 broadcast_in_dim.47
  361.5 30.9 %scatter_fusion = bf16[64,8,320]{2,1,0:T(8,128)(2,1)} fusion(bf16[64,8,320]{2,1,0:T(8,128)(2,1)} %broadcast_in_dim.47, s32[256]{0:T(256)S(1)} %bitcast.42, bf16[256,320]{1,0:T(8,128)(2,1)S(1)} %copy.47), kind=kCustom, calls=%fused_computation | custom fusion | bytes 493568 | tf_op jit(solution)/shard_map/scatter | solution.py:64
  392.4 11.9 %all-to-all-start = ((bf16[64,8,320]{2,1,0:T(8,128)(2,1)}), bf16[64,8,320]{2,1,0:T(8,128)(2,1)S(1)}, u32[]{:S(2)}, u32[]{:S(2)}) async-start(bf16[64,8,320]{2,1,0:T(8,128)(2,1)} %scatter_fusion), calls=%async_computation.2 | async-start | bytes 786432 | tf_op jit(solution)/shard_map/all_to_all | solution.py:63
  404.3 0.0 copy-done.5
  404.3 0.1 multiply_reduce_fusion
  404.4 0.1 and_reduce_fusion
  404.6 60.3 %scatter_custom_fusion.2 = s32[512]{0:T(512)S(1)} fusion(s32[16384]{0:T(1024)S(1)} %bitcast.45, s32[16384]{0:T(1024)S(1)} %bitcast.46, s32[]{:T(128)} %constant.43.clone.1), kind=kCustom, calls=%fused_computation.95 | custom fusion | bytes 2052
  464.9 0.1 reshape.292
  465.0 0.1 copy.43
  465.0 0.1 reshape.285
  465.1 0.0 all-to-all-done
  465.2 2.6 scatter_custom_fusion.1
  467.7 0.9 copy.49
  (25 shorter events, 0.3 us)
Async XLA Ops:
  6.5 44.2 %all-gather.7.cloned.1.call-start = ((), (), s32[]{:S(2)}) async-start(), calls=%async_computation.3 | async-start | bytes 3276800 | tf_op jit(solution)/shard_map/all_gather | solution.py:10
  7.3 125.7 %all-gather.13.cloned.1.call-start = ((), (), s32[]{:S(2)}) async-start(), calls=%async_computation.8 | async-start | bytes 3993600 | tf_op jit(solution)/shard_map/all_gather | solution.py:19
  8.0 203.7 %all-gather.11.cloned.1.call-start = ((), (), s32[]{:S(2)}) async-start(), calls=%async_computation.7 | async-start | bytes 3993600 | tf_op jit(solution)/shard_map/all_gather | solution.py:18
  8.7 281.6 %all-gather.9.cloned.1.call-start = ((), (), s32[]{:S(2)}) async-start(), calls=%async_computation.5 | async-start | bytes 3993600 | tf_op jit(solution)/shard_map/all_gather | solution.py:20
  9.3 316.6 %reduce-scatter.3.cloned.1.call-start = ((), (), s32[]{:S(2)}) async-start(), calls=%async_computation.4 | async-start | bytes 3276800 | tf_op jit(solution)/shard_map/reduce_scatter | solution.py:25
  50.7 2.5 copy-start
  139.1 78.8 %copy-start.6 = (f32[1280]{0:T(1024)S(1)}, f32[1280]{0:T(1024)}, u32[]{:S(2)}) copy-start(f32[1280]{0:T(1024)} %param.15) | copy-start | bytes 15364
  139.1 78.8 %copy-start.7 = (f32[1280]{0:T(1024)S(1)}, f32[1280]{0:T(1024)}, u32[]{:S(2)}) copy-start(f32[1280]{0:T(1024)} %param.13) | copy-start | bytes 15364
  139.1 78.8 %copy-start.8 = (f32[1280]{0:T(1024)S(1)}, f32[1280]{0:T(1024)}, u32[]{:S(2)}) copy-start(f32[1280]{0:T(1024)} %param.12) | copy-start | bytes 15364
  217.8 21.5 %copy-start.1 = (s32[16384]{0:T(1024)S(1)}, s32[16384]{0:T(1024)}, u32[]{:S(2)}) copy-start(s32[16384]{0:T(1024)} %param.21) | copy-start | bytes 196612
  239.2 86.7 %copy-start.2 = (f32[320]{0:T(512)S(1)}, f32[320]{0:T(512)}, u32[]{:S(2)}) copy-start(f32[320]{0:T(512)} %param.17) | copy-start | bytes 3844
  239.3 120.2 %reduce-scatter.5.cloned.1.call-start = ((), (), s32[]{:S(2)}) async-start(), calls=%async_computation.6 | async-start | bytes 819200 | tf_op jit(solution)/shard_map/reduce_scatter | solution.py:57
  333.1 26.4 %copy-start.3 = (f32[320]{0:T(512)S(1)}, f32[320]{0:T(512)}, u32[]{:S(2)}) copy-start(f32[320]{0:T(512)} %param.19) | copy-start | bytes 3844
  336.4 67.9 %copy-start.5 = (s32[2]{0:T(128)S(1)}, s32[2]{0:T(128)}, u32[]{:S(2)}) copy-start(s32[2]{0:T(128)} %constant.137) | copy-start | bytes 28
  336.4 68.0 %copy-start.4 = (s32[2]{0:T(128)S(1)}, s32[2]{0:T(128)}, u32[]{:S(2)}) copy-start(s32[2]{0:T(128)} %constant.140) | copy-start | bytes 28
  392.4 72.8 %all-to-all-start = ((bf16[64,8,320]{2,1,0:T(8,128)(2,1)}), bf16[64,8,320]{2,1,0:T(8,128)(2,1)S(1)}, u32[]{:S(2)}, u32[]{:S(2)}) async-start(bf16[64,8,320]{2,1,0:T(8,128)(2,1)} %scatter_fusion), calls=%async_computation.2 | async-start | bytes 786432 | tf_op jit(solution)/shard_map/all_to_all | solution.py:63
Sparse Core Ops, SparseCore 0:
  9.2 41.5 all-gather.6
  53.4 79.4 all-gather.12
  135.6 76.0 all-gather.10
  214.3 75.9 all-gather.8
  292.7 33.2 reduce-scatter.2
  336.5 22.9 reduce-scatter.4
where the time goes:
time: 477 us; the launch traced here: 475 us
  waiting for transfers between devices  294 us (62%)
  local copies, waits for them, and re-layouts  122 us (26%)
  matrix products  24.7 us (5%)
  between operations  13.7 us (3%)
  starting transfers between devices  12.1 us (3%)
  other arithmetic  8.4 us (2%)
    all_gather x1, waiting for transfers between devices, per_device(): lax.all_gather(w_out, 'wide', axis=1, tiled=True)  78.9 us
    unnamed x25, local copies, waits for them, and re-layouts  74.1 us
    all_gather x1, waiting for transfers between devices, per_device(): lax.all_gather(w_in, 'wide', axis=0, tiled=True)  72.6 us
    all_gather x1, waiting for transfers between devices, per_device(): lax.all_gather(w_proj, 'wide', axis=2, tiled=True)  49.9 us
    all_gather x1, waiting for transfers between devices, per_device(): whole = lax.all_gather(patches, 'narrow', axis=1, tiled=True)  41.4 us
    scatter x1, local copies, waits for them, and re-layouts, per_device(): buffer.at[own_owners, slot_out].set(vision, mode='drop')  30.9 us
    reduce_scatter x1, waiting for transfers between devices, per_device(): lax.psum_scatter(partial_out.astype(jnp.bfloat16), 'narrow', scatter_dime...  28.3 us
    dot_general x1, matrix products, per_device(): partial_out = jnp.dot(hidden, cols_out, preferred_element_type=jnp.float32)  21.4 us
  transfers between devices with their start and end apart: 7, of which 6 were waited for; matrix products, arithmetic and copies ran while one was open for 23% of the time, Pallas kernels for 0%

commit v1 on v0

--- a/solution.py
+++ b/solution.py
@@ -7,7 +7,22 @@
 def per_device(
     patches, norm_gain, norm_bias, w_in, b_in, w_out, b_out, w_proj, b_proj, text, place
 ):
-    whole = lax.all_gather(patches, "narrow", axis=1, tiled=True)
+    ways, here, step = (lax.axis_size("narrow"), lax.axis_index("narrow"), patches.shape[1])
+    lengths = [n * ways if d == 1 else n for d, n in enumerate(patches.shape)]
+    whole = lax.dynamic_update_slice_in_dim(
+        jnp.zeros(lengths, patches.dtype), patches, here * step, axis=1
+    )
+    going_up = going_down = patches
+    for far in range(1, ways // 2 + 1):
+        going_up = lax.ppermute(going_up, "narrow", [(d, (d + 1) % ways) for d in range(ways)])
+        whole = lax.dynamic_update_slice_in_dim(whole, going_up, (here - far) % ways * step, axis=1)
+        if 2 * far < ways:
+            going_down = lax.ppermute(
+                going_down, "narrow", [(d, (d - 1) % ways) for d in range(ways)]
+            )
+            whole = lax.dynamic_update_slice_in_dim(
+                whole, going_down, (here + far) % ways * step, axis=1
+            )
     values = whole.astype(jnp.float32)
     center = jnp.mean(values, axis=-1, keepdims=True)
     spread = jnp.mean(jnp.square(values - center), axis=-1, keepdims=True)

time: 477 us -> 438 us (0.918)
  waiting for transfers between devices: 294 us -> 247 us
  starting transfers between devices: 12.1 us -> 17.5 us
    all_gather x1 -> x0, waiting for transfers between devices: 41.4 us -> none  [per_device(): whole = lax.all_gather(patches, 'narrow', axis=1, tiled=True)]
    ppermute x0 -> x3, waiting for transfers between devices: none -> 23.2 us  [the longest x2 23.2 us: per_device(): lax.ppermute(going_up, 'narrow', [(d, (d + 1) % ways) for d in range(ways)])]
    all_gather x1, waiting for transfers between devices: 72.6 us -> 51.3 us  [per_device(): lax.all_gather(w_in, 'wide', axis=0, tiled=True)]
    all_gather x1, waiting for transfers between devices: 78.9 us -> 72.6 us  [per_device(): lax.all_gather(w_out, 'wide', axis=1, tiled=True)]
    ppermute x0 -> x3, starting transfers between devices: none -> 5.46 us  [the longest x2 4.1 us: per_device(): lax.ppermute(going_up, 'narrow', [(d, (d + 1) % ways) for d in range(ways)])]
    unnamed x25 -> x29, local copies, waits for them, and re-layouts: 74.1 us -> 73.5 us
  transfers between devices with their start and end apart: 7 -> 9, of which waited for: 6 -> 7; matrix products, arithmetic and copies ran while one was open for 23% -> 25% of each run, Pallas kernels for 0% -> 0%
where the time goes in v1:
time: 438 us; the launch traced here: 436 us
  waiting for transfers between devices  247 us (56%)
  local copies, waits for them, and re-layouts  125 us (29%)
  matrix products  24.7 us (6%)
  starting transfers between devices  17.5 us (4%)
  between operations  13.5 us (3%)
  other arithmetic  7.2 us (2%)
    unnamed x29, local copies, waits for them, and re-layouts  73.5 us
    all_gather x1, waiting for transfers between devices, per_device(): lax.all_gather(w_out, 'wide', axis=1, tiled=True)  72.6 us
    all_gather x1, waiting for transfers between devices, per_device(): lax.all_gather(w_in, 'wide', axis=0, tiled=True)  51.3 us
    all_gather x1, waiting for transfers between devices, per_device(): lax.all_gather(w_proj, 'wide', axis=2, tiled=True)  49.5 us
    scatter x1, local copies, waits for them, and re-layouts, per_device(): buffer.at[own_owners, slot_out].set(vision, mode='drop')  30.9 us
    reduce_scatter x1, waiting for transfers between devices, per_device(): lax.psum_scatter(partial_out.astype(jnp.bfloat16), 'narrow', scatter_dime...  28.3 us
    ppermute x2, waiting for transfers between devices, per_device(): lax.ppermute(going_up, 'narrow', [(d, (d + 1) % ways) for d in range(ways)])  23.2 us
    dot_general x1, matrix products, per_device(): partial_out = jnp.dot(hidden, cols_out, preferred_element_type=jnp.float32)  21.4 us
  transfers between devices with their start and end apart: 9, of which 7 were waited for; matrix products, arithmetic and copies ran while one was open for 25% of the time, Pallas kernels for 0%

profile of v1, /device:TPU:1, one launch (start us, length us, event | category | flops | bytes accessed | tf_op | source)
XLA Modules:
  0.0 435.8 jit_solution(3164539652179490823)
XLA Ops:
  6.5 0.7 all-gather.8.cloned.1.call-update
  7.3 0.0 all-gather.10.cloned.1.call-start
  7.3 0.7 all-gather.10.cloned.1.call-update
  8.0 0.0 all-gather.6.cloned.1.call-start
  8.1 2.1 collective-permute-start
  10.2 1.4 collective-permute-start.1
  11.5 12.3 %collective-permute-done = bf16[1024,320]{0,1:T(8,128)(2,1)S(1)} collective-permute-done((bf16[1024,320]{0,1:T(8,128)(2,1)}, bf16[1024,320]{0,1:T(8,128)(2,1)S(1)}, u32[]{:S(2)}, u32[]{:S(2)}) %collective-permute-start) | collective-permute-done | bytes 655392 | tf_op jit(solution)/shard_map/ppermute | solution.py:17
  23.8 2.0 collective-permute-start.2
  25.8 0.0 all-gather.6.cloned.1.call-update
  25.8 0.0 reduce-scatter.3.cloned.1.call-start
  25.9 0.3 broadcast_in_dim.52
  26.3 1.1 constant_dynamic-update-slice_fusion.3
  27.4 0.1 constant_dynamic-update-slice_fusion.2
  27.5 1.1 constant_dynamic-update-slice_fusion.1
  28.6 10.9 %collective-permute-done.2 = bf16[1024,320]{0,1:T(8,128)(2,1)} collective-permute-done((bf16[1024,320]{0,1:T(8,128)(2,1)S(1)}, bf16[1024,320]{0,1:T(8,128)(2,1)}, u32[]{:S(2)}, u32[]{:S(2)}) %collective-permute-start.2) | collective-permute-done | bytes 655392 | tf_op jit(solution)/shard_map/ppermute | solution.py:17
  39.6 1.1 constant_dynamic-update-slice_fusion
  40.7 0.5 convert_reduce_fusion
  41.2 0.7 fusion.2
  41.9 51.3 %all-gather.8.cloned.1.call-done = bf16[64,20,1280]{2,1,0:T(8,128)(2,1)} async-done(((bf16[1,20,1280]{2,1,0:T(8,128)(2,1)}), bf16[64,20,1280]{2,1,0:T(8,128)(2,1)}) %all-gather.8.cloned.1.call-update) | async-done | bytes 3276816 | tf_op jit(solution)/shard_map/all_gather | solution.py:33
  93.2 6.1 %reshape.315 = bf16[1280,1280]{1,0:T(8,128)(2,1)} reshape(bf16[64,20,1280]{2,1,0:T(8,128)(2,1)} %all-gather.8.cloned.1.call-done) | data formatting | bytes 6553600
  99.3 72.6 %all-gather.10.cloned.1.call-done = bf16[64,20,1280]{2,1,0:T(8,128)(2,1)} async-done(((bf16[1,20,1280]{2,1,0:T(8,128)(2,1)}), bf16[64,20,1280]{2,1,0:T(8,128)(2,1)}) %all-gather.10.cloned.1.call-update) | async-done | bytes 3276816 | tf_op jit(solution)/shard_map/all_gather | solution.py:34
  172.0 6.1 %reshape.317 = bf16[1280,1280]{1,0:T(8,128)(2,1)} reshape(bf16[64,20,1280]{2,1,0:T(8,128)(2,1)} %all-gather.10.cloned.1.call-done) | data formatting | bytes 6553600
  178.1 0.0 copy-start
  178.1 21.4 %convolution_convert_fusion = bf16[1024,1280]{0,1:T(8,128)(2,1)} fusion(bf16[1280,1280]{1,0:T(8,128)(2,1)} %reshape.317, bf16[1280,1280]{1,0:T(8,128)(2,1)} %reshape.315, bf16[1024,1280]{0,1:T(8,128)(2,1)S(1)} %constant_dynamic-update-slice_fusion, f32[1280]{0:T(1024)S(1)} %copy-done.8, f32[1280]{0:T(1024)S(1)} %copy-done.9, f32[1280]{0:T(1024)S(1)} %copy-done.10, ...), kind=kOutput, calls=%fused_computation.30 | convolution fusion | flops 6806568960 | bytes 11820032 | tf_op jit(solution)/shard_map/dot_general | solution.py:39
  199.5 0.0 reduce-scatter.3.cloned.1.call-update
  199.5 0.0 reduce-scatter.5.cloned.1.call-start
  199.6 0.0 copy-start.4
  199.7 0.1 fusion.31
  199.8 0.0 copy-start.2
  199.8 0.6 copy-done.2
  200.4 0.6 reduce-window.16
  201.0 0.2 slice_reduce_fusion
  201.2 49.5 %all-gather.6.cloned.1.call-done = bf16[4,320,1280]{1,0,2:T(4,128)(2,1)} async-done(((bf16[4,320,20]{1,0,2:T(4,128)(2,1)}), bf16[4,320,1280]{1,0,2:T(4,128)(2,1)}) %all-gather.6.cloned.1.call-update) | async-done | bytes 3276816 | tf_op jit(solution)/shard_map/all_gather | solution.py:35
  250.7 7.3 %copy.46 = bf16[4,320,1280]{2,1,0:T(8,128)(2,1)S(1)} copy(bf16[4,320,1280]{1,0,2:T(4,128)(2,1)} %all-gather.6.cloned.1.call-done) | data formatting | bytes 6553600 | tf_op jit(solution)/shard_map/all_gather | solution.py:35
  258.1 28.3 %reduce-scatter.3.cloned.1.call-done = bf16[1024,320]{0,1:T(8,128)(2,1)} async-done(((bf16[1024,1280]{0,1:T(8,128)(2,1)}), bf16[1024,320]{0,1:T(8,128)(2,1)}) %reduce-scatter.3.cloned.1.call-update) | async-done | bytes 655376 | tf_op jit(solution)/shard_map/reduce_scatter | solution.py:40
  286.4 2.4 add_convert_fusion
  288.8 2.2 copy.45
  291.0 2.5 reshape.287
  293.6 3.3 convolution_convert_fusion.1
  296.9 0.0 reduce-scatter.5.cloned.1.call-update
  296.9 0.1 fusion.40
  296.9 0.6 reduce-window.14
  297.6 0.2 slice_reduce_fusion.1
  297.8 0.1 add_add_fusion
  297.9 0.1 copy.42
  297.9 0.1 sub.43
  298.0 0.1 fusion.35
  298.1 0.7 or_select_fusion
  298.8 0.1 compare_select_fusion
  298.9 21.0 %reduce-scatter.5.cloned.1.call-done = bf16[256,320]{0,1:T(8,128)(2,1)} async-done(((bf16[256,1280]{0,1:T(8,128)(2,1)}), bf16[256,320]{0,1:T(8,128)(2,1)}) %reduce-scatter.5.cloned.1.call-update) | async-done | bytes 163856 | tf_op jit(solution)/shard_map/reduce_scatter | solution.py:72
  319.9 1.0 add_convert_fusion.1
  321.0 0.2 copy.47
  321.1 0.8 broadcast_in_dim.50
  321.9 30.9 %scatter_fusion = bf16[64,8,320]{2,1,0:T(8,128)(2,1)} fusion(bf16[64,8,320]{2,1,0:T(8,128)(2,1)} %broadcast_in_dim.50, s32[256]{0:T(256)S(1)} %bitcast.42, bf16[256,320]{1,0:T(8,128)(2,1)S(1)} %copy.47), kind=kCustom, calls=%fused_computation | custom fusion | bytes 493568 | tf_op jit(solution)/shard_map/scatter | solution.py:79
  352.8 11.9 %all-to-all-start = ((bf16[64,8,320]{2,1,0:T(8,128)(2,1)}), bf16[64,8,320]{2,1,0:T(8,128)(2,1)S(1)}, u32[]{:S(2)}, u32[]{:S(2)}) async-start(bf16[64,8,320]{2,1,0:T(8,128)(2,1)} %scatter_fusion), calls=%async_computation.2 | async-start | bytes 786432 | tf_op jit(solution)/shard_map/all_to_all | solution.py:78
  364.7 0.1 multiply_reduce_fusion
  364.8 0.1 and_reduce_fusion
  365.0 60.3 %scatter_custom_fusion.2 = s32[512]{0:T(512)S(1)} fusion(s32[16384]{0:T(1024)S(1)} %bitcast.45, s32[16384]{0:T(1024)S(1)} %bitcast.46, s32[]{:T(128)} %constant.49.clone.1), kind=kCustom, calls=%fused_computation.100 | custom fusion | bytes 2052
  425.3 0.1 reshape.292
  425.4 0.1 copy.43
  425.5 0.1 reshape.285
  425.6 0.2 copy.48
  425.8 2.6 scatter_custom_fusion.1
  428.4 0.9 copy.49
  (38 shorter events, 0.3 us)
Async XLA Ops:
  6.5 86.7 %all-gather.8.cloned.1.call-start = ((), (), s32[]{:S(2)}) async-start(), calls=%async_computation.6 | async-start | bytes 3993600 | tf_op jit(solution)/shard_map/all_gather | solution.py:33
  7.3 164.7 %all-gather.10.cloned.1.call-start = ((), (), s32[]{:S(2)}) async-start(), calls=%async_computation.7 | async-start | bytes 3993600 | tf_op jit(solution)/shard_map/all_gather | solution.py:34
  8.0 242.7 %all-gather.6.cloned.1.call-start = ((), (), s32[]{:S(2)}) async-start(), calls=%async_computation.4 | async-start | bytes 3993600 | tf_op jit(solution)/shard_map/all_gather | solution.py:35
  8.1 15.8 %collective-permute-start = (bf16[1024,320]{0,1:T(8,128)(2,1)}, bf16[1024,320]{0,1:T(8,128)(2,1)S(1)}, u32[]{:S(2)}, u32[]{:S(2)}) collective-permute-start(bf16[1024,320]{0,1:T(8,128)(2,1)} %param.11), channel_id=1, source_target_pairs={{0,1},{1,2},{2,3},{3,0},{4,5},{5,6},{6,7},{7,4},{8,9},{9,10},{10,1... | collective-permute-start | bytes 1966088 | tf_op jit(solution)/shard_map/ppermute | solution.py:17
  10.2 17.3 %collective-permute-start.1 = (bf16[1024,320]{0,1:T(8,128)(2,1)}, bf16[1024,320]{0,1:T(8,128)(2,1)}, u32[]{:S(2)}, u32[]{:S(2)}) collective-permute-start(bf16[1024,320]{0,1:T(8,128)(2,1)} %param.11), channel_id=1, source_target_pairs={{0,3},{1,0},{2,1},{3,2},{4,7},{5,4},{6,5},{7,6},{8,11},{9,8},{10,9... | collective-permute-start | bytes 1966088 | tf_op jit(solution)/shard_map/ppermute | solution.py:20
  23.8 15.7 %collective-permute-start.2 = (bf16[1024,320]{0,1:T(8,128)(2,1)S(1)}, bf16[1024,320]{0,1:T(8,128)(2,1)}, u32[]{:S(2)}, u32[]{:S(2)}) collective-permute-start(bf16[1024,320]{0,1:T(8,128)(2,1)S(1)} %collective-permute-done), channel_id=1, source_target_pairs={{0,1},{1,2},{2,3},{3,0},{4,5},{5,6},{6,7},{7,4},{8,9},{9,10},{10,1... | collective-permute-start | bytes 1966088 | tf_op jit(solution)/shard_map/ppermute | solution.py:17
  25.8 260.6 %reduce-scatter.3.cloned.1.call-start = ((), (), s32[]{:S(2)}) async-start(), calls=%async_computation.3 | async-start | bytes 3276800 | tf_op jit(solution)/shard_map/reduce_scatter | solution.py:40
  99.3 78.7 %copy-start.8 = (f32[1280]{0:T(1024)S(1)}, f32[1280]{0:T(1024)}, u32[]{:S(2)}) copy-start(f32[1280]{0:T(1024)} %param.15) | copy-start | bytes 15364
  99.3 78.7 %copy-start.9 = (f32[1280]{0:T(1024)S(1)}, f32[1280]{0:T(1024)}, u32[]{:S(2)}) copy-start(f32[1280]{0:T(1024)} %param.13) | copy-start | bytes 15364
  99.3 78.7 %copy-start.10 = (f32[1280]{0:T(1024)S(1)}, f32[1280]{0:T(1024)}, u32[]{:S(2)}) copy-start(f32[1280]{0:T(1024)} %param.12) | copy-start | bytes 15364
  178.1 21.5 %copy-start = (s32[16384]{0:T(1024)S(1)}, s32[16384]{0:T(1024)}, u32[]{:S(2)}) copy-start(s32[16384]{0:T(1024)} %param.21) | copy-start | bytes 196612
  199.5 120.4 %reduce-scatter.5.cloned.1.call-start = ((), (), s32[]{:S(2)}) async-start(), calls=%async_computation.5 | async-start | bytes 819200 | tf_op jit(solution)/shard_map/reduce_scatter | solution.py:72
  199.6 86.8 %copy-start.4 = (f32[320]{0:T(512)S(1)}, f32[320]{0:T(512)}, u32[]{:S(2)}) copy-start(f32[320]{0:T(512)} %param.17) | copy-start | bytes 3844
  199.8 0.6 copy-start.2
  201.2 87.6 %copy-start.3 = (s32[64,3]{0,1:T(4,128)}, s32[64,3]{0,1:T(4,128)S(1)}, u32[]{:S(2)}) copy-start(s32[64,3]{0,1:T(4,128)S(1)} %reduce-window.19) | copy-start | bytes 2308
  291.0 7.0 %slice-start = ((s32[64,3]{0,1:T(4,128)}), s32[64,2]{0,1:T(2,128)S(1)}, s32[]{:S(2)}) async-start(s32[64,3]{0,1:T(4,128)} %copy-done.3), calls=%async_computation.8 | async-start | bytes 2048 | tf_op jit(solution)/shard_map/slice.3
  293.6 26.4 %copy-start.5 = (f32[320]{0:T(512)S(1)}, f32[320]{0:T(512)}, u32[]{:S(2)}) copy-start(f32[320]{0:T(512)} %param.19) | copy-start | bytes 3844
  296.9 67.9 %copy-start.7 = (s32[2]{0:T(128)S(1)}, s32[2]{0:T(128)}, u32[]{:S(2)}) copy-start(s32[2]{0:T(128)} %constant.170) | copy-start | bytes 28
  296.9 68.0 %copy-start.6 = (s32[2]{0:T(128)S(1)}, s32[2]{0:T(128)}, u32[]{:S(2)}) copy-start(s32[2]{0:T(128)} %constant.173) | copy-start | bytes 28
  296.9 128.7 %copy-start.1 = (bf16[512,320]{0,1:T(8,128)(2,1)S(1)}, bf16[512,320]{0,1:T(8,128)(2,1)}, u32[]{:S(2)}) copy-start(bf16[512,320]{0,1:T(8,128)(2,1)} %param.20) | copy-start | bytes 983044
  352.8 73.0 %all-to-all-start = ((bf16[64,8,320]{2,1,0:T(8,128)(2,1)}), bf16[64,8,320]{2,1,0:T(8,128)(2,1)S(1)}, u32[]{:S(2)}, u32[]{:S(2)}) async-start(bf16[64,8,320]{2,1,0:T(8,128)(2,1)} %scatter_fusion), calls=%async_computation.2 | async-start | bytes 786432 | tf_op jit(solution)/shard_map/all_to_all | solution.py:78
Sparse Core Ops, SparseCore 0:
  10.0 83.1 all-gather.7
  95.9 76.0 all-gather.9
  174.7 76.0 all-gather.5
  253.1 33.2 reduce-scatter.2
  297.0 22.8 reduce-scatter.4
